TPU v7x, 32 devices: a whole 2x2x4 slice. The times are simulated.
32 devices in a mesh: grp: 4 (over z), mem: 8 (over y, x, core).
Axes of the slice: x: 2, y: 2, z: 4, core: 2. Of those that a mesh axis runs over, the one named last changes fastest.
Arguments:
- embeddings: bfloat16 [32768, 4096], P(('grp', 'mem')), may hold values from -6 to 6
- local_picks: int32 [4, 64], P('grp', 'mem'), may hold values from 0 to 1023
- second_picks: int32 [4, 16], P('grp'), may hold values from 0 to 63
- final_picks: int32 [16], replicated, may hold values from 0 to 63
Outputs:
- gain_table: float32 [64, 64], P('grp', 'mem')
- final_cover: float32 [32768], P(('grp', 'mem'))
Inputs may be any that keep to these rules, and one draw needn't show every extreme that they name: `local_picks`: entry (g, m * 8 + k) names a row among the 1024 points of device m of group g; repeats may occur. `second_picks`: candidate indices of the group, in greedy order; repeats may occur. `final_picks`: index g * 16 + t names group g's second-round pick t; repeats may occur.
All inputs are finite; a program needn't handle non-finite values.
Results may differ from a plain program's by a relative error of at most 0.0003.
Values may be sent and summed in bfloat16 or wider, within the bound.
No kernel may reach another device: no remote copies, remote signals or barrier semaphores. Data moves between devices by JAX's collectives and lax.ppermute only.
A program may use at most 64 MiB of HBM per device.

v0:
```python
import jax
import jax.numpy as jnp
from jax import lax
from jax.sharding import PartitionSpec as P

D = 4096


def per_device(embeddings, local_picks, second_picks, final_picks):
    scaling = float(D) ** (-0.5)
    point_count = embeddings.shape[0]
    local_count = local_picks.shape[1]
    second_list = second_picks[0]
    member = lax.axis_index("mem")
    choose = (local_picks[0][:, None] == lax.iota(jnp.int32, point_count)[None, :]).astype(
        jnp.bfloat16
    )
    own_rows = jnp.dot(choose, embeddings, preferred_element_type=jnp.float32).astype(jnp.bfloat16)

    def similar(other_rows):
        dims = (((1,), (1,)), ((), ()))
        return (
            lax.dot_general(embeddings, other_rows, dims, preferred_element_type=jnp.float32)
            * scaling
        )

    candidates = lax.all_gather(own_rows, "mem", axis=0, tiled=True)
    similar_map = similar(candidates)
    cand_total = candidates.shape[0]
    pick_table = (second_list[:, None] == lax.iota(jnp.int32, cand_total)[None, :]).astype(
        jnp.bfloat16
    )
    winners = jnp.dot(pick_table, candidates, preferred_element_type=jnp.float32).astype(
        jnp.bfloat16
    )
    union_rows = lax.all_gather(winners, "grp", axis=0, tiled=True)
    final_table = (
        final_picks[:, None] == lax.iota(jnp.int32, union_rows.shape[0])[None, :]
    ).astype(jnp.bfloat16)
    final_rows = jnp.dot(final_table, union_rows, preferred_element_type=jnp.float32).astype(
        jnp.bfloat16
    )
    own_block = lax.dynamic_slice_in_dim(similar_map, member * local_count, local_count, 1)
    coverage = jnp.max(own_block, axis=1)
    chosen_cols = jnp.take(similar_map, second_list, axis=1)

    def greedy_step(cover_now, column):
        partial_value = jnp.sum(jnp.maximum(similar_map - cover_now[:, None], 0.0), axis=0)
        return (jnp.maximum(cover_now, column), partial_value)

    _, partials = lax.scan(greedy_step, coverage, chosen_cols.T)
    gain_table = lax.psum_scatter(partials, "mem", scatter_dimension=1, tiled=True) / point_count
    final_cover = jnp.max(similar(final_rows), axis=1)
    return (gain_table, final_cover)


def solution(mesh):
    placed = (P(("grp", "mem"), None), P("grp", "mem"), P("grp", None), P())
    return jax.shard_map(
        per_device,
        mesh=mesh,
        in_specs=placed,
        out_specs=(P("grp", "mem"), P(("grp", "mem"))),
        check_vma=False,
    )
```

profile of v0, /device:TPU:0, one launch (start us, length us, event | category | flops | bytes accessed | tf_op | source)
XLA Modules:
  0.0 75.5 jit_solution(6943562138550951512)
XLA Ops:
  0.6 1.2 %dynamic-slice.4 = u32[1]{0:T(128)} dynamic-slice(u32[32]{0:T(128)} %constant.50, u32[]{:T(128)S(6)} %add.27), dynamic_slice_sizes={1} | dynamic-slice | bytes 12
  2.5 0.7 compare_and_fusion
  3.2 0.7 fusion.7
  3.9 4.8 %convolution_convert_fusion.2 = bf16[8,4096]{1,0:T(8,128)(2,1)S(1)} fusion(bf16[1024,4096]{1,0:T(8,128)(2,1)} %param.6, s32[8]{0:T(128)} %bitcast.25), kind=kOutput, calls=%fused_computation.5 | convolution fusion | flops 67149824 | bytes 8454176 | tf_op jit(solution)/shard_map/dot_general | solution.py:18
  8.7 11.3 %all_gather.6 = bf16[64,4096]{1,0:T(8,128)(2,1)S(1)} all-gather(bf16[8,4096]{1,0:T(8,128)(2,1)S(1)} %convolution_convert_fusion.2), channel_id=1, replica_groups=mesh['grp'=4,'mem'=8] {'mem'}, dimensions={0}, use_global_device_ids=true | all-gather | bytes 589824 | tf_op jit(solution)/shard_map/all_gather | solution.py:27
  20.0 0.2 convolution_convert_fusion.1
  20.3 2.7 %convolution_multiply_fusion = f32[64,1024]{1,0:T(8,128)S(1)} fusion(bf16[64,4096]{1,0:T(8,128)(2,1)S(1)} %all_gather.6, bf16[1024,4096]{1,0:T(8,128)(2,1)S(1)} %copy-done), kind=kOutput, calls=%fused_computation.6 | convolution fusion | flops 536936448 | bytes 9175040 | tf_op jit(solution)/shard_map/dot_general | solution.py:23
  23.0 0.6 gather_fusion
  23.5 0.1 broadcast_select_fusion
  23.6 0.2 copy.8
  23.8 4.8 %while.12 = (s32[]{:T(128)}, f32[1024]{0:T(1024)S(1)}, f32[16,64]{1,0:T(8,128)S(1)}, f32[16,1024]{1,0:T(8,128)S(1)}, f32[1024,64]{1,0:T(8,128)S(1)}, /*index=5*/s32[]{:T(128)}, s32[]{:T(128)}) while((s32[]{:T(128)}, f32[1024]{0:T(1024)S(1)}, f32[16,64]{1,0:T(8,128)S(1)}, f32[16,1024]{1,0:T(8,128)S(1)}, f32[1024,64]{1,0:T(8,128)S(1)}, ...), condition=%wide.region_3.4_spmd, body=%wide.region_1.0_spmd.sunk | while | flops 197570 | bytes 287581 | solution.py:51
  23.8 0.2 maximum_reduce_fusion.2
  24.1 0.2 maximum_reduce_fusion.2
  24.4 0.2 maximum_reduce_fusion.2
  24.7 0.2 maximum_reduce_fusion.2
  25.0 0.2 maximum_reduce_fusion.2
  25.3 0.2 maximum_reduce_fusion.2
  25.6 0.2 maximum_reduce_fusion.2
  25.9 0.2 maximum_reduce_fusion.2
  26.2 0.2 maximum_reduce_fusion.2
  26.5 0.2 maximum_reduce_fusion.2
  26.8 0.2 maximum_reduce_fusion.2
  27.1 0.2 maximum_reduce_fusion.2
  27.5 0.2 maximum_reduce_fusion.2
  27.8 0.2 maximum_reduce_fusion.2
  28.1 0.2 maximum_reduce_fusion.2
  28.4 0.2 maximum_reduce_fusion.2
  28.7 0.1 copy.9
  28.7 23.6 %all-reduce = f32[16,64]{0,1:T(8,128)S(1)} all-reduce(f32[16,64]{0,1:T(8,128)S(1)} %copy.9), channel_id=2, replica_groups=mesh['grp'=4,'mem'=8] {'mem'}, use_global_device_ids=true, to_apply=%region_4.5.clone | all-reduce | flops 1024 | bytes 8192
  52.3 0.6 dynamic-slice_multiply_fusion
  52.9 16.2 %all_gather.7 = bf16[64,4096]{1,0:T(8,128)(2,1)S(1)} all-gather(bf16[16,4096]{1,0:T(8,128)(2,1)S(1)} %convolution_convert_fusion.1), channel_id=1, replica_groups=mesh['grp'=4,'mem'=8] {'grp'}, dimensions={0}, use_global_device_ids=true | all-gather | bytes 655360 | tf_op jit(solution)/shard_map/all_gather | solution.py:36
  69.1 6.4 %fusion.2 = f32[1024]{0:T(1024)} fusion(bf16[1024,4096]{1,0:T(8,128)(2,1)} %param.6, bf16[64,4096]{1,0:T(8,128)(2,1)S(1)} %all_gather.7, s32[16]{0:T(128)S(1)} %copy-done.1), kind=kOutput, calls=%fused_computation.9 | convolution fusion | flops 142704640 | bytes 8917056 | tf_op jit(solution)/shard_map/dot_general | solution.py:23
  (57 shorter events, 0.9 us)
Async XLA Ops:
  0.6 19.4 %copy-start.2 = (s32[1,16]{1,0:T(1,128)S(1)}, s32[1,16]{1,0:T(1,128)}, u32[]{:S(2)}) copy-start(s32[1,16]{1,0:T(1,128)} %param.8) | copy-start | bytes 196
  3.9 16.4 %copy-start = (bf16[1024,4096]{1,0:T(8,128)(2,1)S(1)}, bf16[1024,4096]{1,0:T(8,128)(2,1)}, u32[]{:S(2)}) copy-start(bf16[1024,4096]{1,0:T(8,128)(2,1)} %param.6) | copy-start | bytes 25165828
  20.3 48.9 %copy-start.1 = (s32[16]{0:T(128)S(1)}, s32[16]{0:T(128)}, u32[]{:S(2)}) copy-start(s32[16]{0:T(128)} %param.9) | copy-start | bytes 196
where the time goes:
time: 75.8 us; the launch traced here: 75.5 us
  blocking collectives  51.1 us (67%)
  matrix products  14.1 us (19%)
  other arithmetic  5.58 us (7%)
  local copies, waits for them, and re-layouts  2.9 us (4%)
  between operations  1.36 us (2%)
    unnamed x1, blocking collectives  23.6 us
    all_gather x1, blocking collectives, per_device(): union_rows = lax.all_gather(winners, 'grp', axis=0, tiled=True)  16.2 us
    all_gather x1, blocking collectives, per_device(): candidates = lax.all_gather(own_rows, 'mem', axis=0, tiled=True)  11.3 us
    dot_general x2, matrix products, similar(): lax.dot_general(embeddings, other_rows, dims, preferred_element_type=jnp....  9.06 us
    dot_general x1, matrix products, per_device(): jnp.dot(choose, embeddings, preferred_element_type=jnp.float32)  4.78 us
    reduce_sum x16, other arithmetic, greedy_step(): jnp.sum(jnp.maximum(similar_map - cover_now[:, None], 0.0), axis=0)  3.49 us

commit v1 on v0

v1 whole, which is shorter than its diff:
```python
import jax
import jax.numpy as jnp
from jax import lax
from jax.experimental import pallas as pl
from jax.experimental.pallas import tpu as pltpu
from jax.sharding import PartitionSpec as P


BLOCK = 8
LANES = 128
NT = (((1,), (1,)), ((), ()))
VM = pl.BlockSpec(memory_space=pltpu.VMEM)
SM = pl.BlockSpec(memory_space=pltpu.SMEM)
PARAMS = pltpu.CompilerParams(vmem_limit_bytes=16 * 1024 * 1024)


def pick_kernel(picks_ref, emb_ref, out_ref, buf, sems):
    count = out_ref.shape[0]

    def copy(k):
        start = pl.multiple_of((picks_ref[0, k] // BLOCK) * BLOCK, BLOCK)
        return pltpu.make_async_copy(emb_ref.at[pl.ds(start, BLOCK), :], buf.at[k], sems.at[k])

    for k in range(count):
        copy(k).start()
    sub = lax.broadcasted_iota(jnp.int32, (count, 1), 0)
    rows = jnp.zeros(out_ref.shape, jnp.float32)
    for k in range(count):
        copy(k).wait()
        shift = (k - picks_ref[0, k]) % BLOCK
        rows = jnp.where(sub == k, pltpu.roll(buf[k].astype(jnp.float32), shift, 0), rows)
    out_ref[...] = rows.astype(out_ref.dtype)


def pick_rows(embeddings, local_picks):
    count, width = local_picks.shape[1], embeddings.shape[1]
    return pl.pallas_call(
        pick_kernel,
        compiler_params=pltpu.CompilerParams(vmem_limit_bytes=60 * 1024 * 1024),
        out_shape=jax.ShapeDtypeStruct((count, width), embeddings.dtype),
        in_specs=[SM, pl.BlockSpec(memory_space=pl.ANY)],
        out_specs=VM,
        scratch_shapes=[
            pltpu.VMEM((count, BLOCK, width), embeddings.dtype),
            pltpu.SemaphoreType.DMA((count,)),
        ],
    )(local_picks, embeddings)


def column(pick, member, own, n_mem):
    rel = lax.div(pick, own) ^ member
    return ((rel >> 1) + (rel & 1) * (n_mem // 2)) * own + lax.rem(pick, own)


def table_kernel(own, n_mem, ids_ref, second_ref, final_ref, emb_ref, out_ref):
    steps, count = second_ref.shape[1], final_ref.shape[0]
    spot = lax.broadcasted_iota(jnp.int32, out_ref.shape, 0)
    lane = lax.broadcasted_iota(jnp.int32, out_ref.shape, 1)
    want = jnp.full(out_ref.shape, -1, jnp.int32)
    for k in range(count):
        at = final_ref[k]
        col = column(second_ref[0, lax.rem(at, steps)], ids_ref[0], own, n_mem)
        want = jnp.where(spot == k, jnp.where(lax.div(at, steps) == ids_ref[1], col, -1), want)
    out_ref[...] = (want == lane).astype(jnp.float32).astype(out_ref.dtype)


def pick_table(ids, second, final_picks, embeddings, own, n_mem):
    return pl.pallas_call(
        lambda *refs: table_kernel(own, n_mem, *refs),
        compiler_params=PARAMS,
        out_shape=jax.ShapeDtypeStruct((final_picks.shape[0], n_mem * own), embeddings.dtype),
        in_specs=[SM, SM, SM, VM],
        out_specs=VM,
    )(ids, second, final_picks, embeddings)


def gain_kernel(n_blocks, scaling, ids_ref, second_ref, emb_ref, *refs):
    blocks, outs, sim_ref = refs[:n_blocks], refs[n_blocks:-1], refs[-1]
    own = blocks[0].shape[0]
    cands, points = sim_ref.shape
    steps = second_ref.shape[1]
    rows = jnp.concatenate([b[...] for b in blocks], 0)
    sim_ref[...] = lax.dot_general(rows, emb_ref[...], NT, preferred_element_type=jnp.float32) * scaling
    cover = jnp.max(sim_ref[0:own, :], axis=0, keepdims=True)
    lane = lax.broadcasted_iota(jnp.int32, (cands, steps), 1)
    result = jnp.zeros((cands, steps), jnp.float32)
    for t in range(steps):
        total = jnp.zeros((cands, LANES), jnp.float32)
        for at in range(0, points, LANES):
            part = slice(at, at + LANES)
            total = total + jnp.maximum(sim_ref[:, part] - cover[:, part], 0.0)
        summed = jnp.sum(total, axis=1, keepdims=True)
        result = jnp.where(lane == t, summed, result)
        col = column(second_ref[0, t], ids_ref[0], own, n_blocks)
        cover = jnp.maximum(cover, sim_ref[pl.ds(col, 1), :])
    each = cands // len(outs)
    for i, out in enumerate(outs):
        out[...] = result[i * each : (i + 1) * each]


def gains(ids, second, embeddings, blocks, scaling):
    n, own = len(blocks), blocks[0].shape[0]
    points, width = embeddings.shape
    steps = second.shape[1]
    body = lambda *refs: gain_kernel(n, scaling, *refs)
    return pl.pallas_call(
        body,
        compiler_params=PARAMS,
        out_shape=[jax.ShapeDtypeStruct((n * own // 2, steps), jnp.float32)] * 2,
        in_specs=[SM, SM] + [VM] * (n + 1),
        out_specs=[VM, VM],
        scratch_shapes=[pltpu.VMEM((n * own, points), jnp.float32)],
        cost_estimate=pl.CostEstimate(
            flops=8 * 2 * n * own * points * width, transcendentals=0, bytes_accessed=2 * embeddings.size
        ),
    )(ids, second, embeddings, *blocks)


def final_kernel(scaling, ids_ref, mine_ref, other_ref, emb_ref, out_ref, rows_ref):
    half = mine_ref.shape[1]
    core = ids_ref[0] & 1
    rows_ref[:, pl.ds(pl.multiple_of(core * half, LANES), half)] = mine_ref[...]
    rows_ref[:, pl.ds(pl.multiple_of((1 - core) * half, LANES), half)] = other_ref[...]
    sim = lax.dot_general(rows_ref[...], emb_ref[...], NT, preferred_element_type=jnp.float32)
    out_ref[...] = jnp.max(sim * scaling, axis=0)


def final(ids, mine, other, embeddings, scaling):
    count, _ = mine.shape
    points, width = embeddings.shape
    body = lambda *refs: final_kernel(scaling, *refs)
    return pl.pallas_call(
        body,
        compiler_params=PARAMS,
        out_shape=jax.ShapeDtypeStruct((points,), jnp.float32),
        in_specs=[SM] + [VM] * 3,
        out_specs=VM,
        scratch_shapes=[pltpu.VMEM((count, width), mine.dtype)],
        cost_estimate=pl.CostEstimate(
            flops=8 * 2 * 64 * points * width, transcendentals=0, bytes_accessed=2 * embeddings.size
        ),
    )(ids, mine, other, embeddings)


def build(n_grp, n_mem):
    def swap(x, axis, size, mask):
        return lax.ppermute(x, axis, [(i, i ^ mask) for i in range(size)])

    masks = [1 << b for b in range(1, n_mem.bit_length() - 1)]
    rounds = []
    for at in range(0, len(masks), 2):
        pair = masks[at : at + 2]
        rounds.append(pair + ([pair[0] ^ pair[1]] if len(pair) == 2 else []))

    def per_device(embeddings, local_picks, second_picks, final_picks):
        points, width = embeddings.shape
        scaling = float(width) ** -0.5
        own = local_picks.shape[1]
        half_count = n_mem // 2
        order = [2 * i for i in range(half_count)] + [2 * i + 1 for i in range(half_count)]
        member = lax.axis_index("mem").astype(jnp.int32)
        ids = jnp.stack([member, lax.axis_index("grp").astype(jnp.int32)])
        side = (member & 1) * (width // 2)
        picks, ids, side = lax.optimization_barrier((local_picks, ids, side))

        blocks = {0: pick_rows(embeddings, picks)}
        table = pick_table(ids, second_picks, final_picks, embeddings, own, n_mem)
        emb = embeddings
        for reach in rounds:
            held = sorted(blocks)
            for mask in reach:
                for j in held:
                    blocks[j ^ mask] = swap(blocks[j], "mem", n_mem, mask)
        for j in sorted(blocks):
            blocks[j ^ 1] = swap(blocks[j], "mem", n_mem, 1)
        ordered = [blocks[j] for j in order]

        part = lax.dynamic_slice_in_dim(
            jnp.concatenate(ordered, 0), side, width // 2, 1
        )
        final_half = jnp.dot(table, part, preferred_element_type=jnp.float32).astype(emb.dtype)
        others = [swap(final_half, "grp", n_grp, g) for g in range(1, n_grp)]
        final_half = sum(others, final_half)

        keep, send = gains(ids, second_picks, emb, ordered, scaling)
        final_other = swap(final_half, "mem", n_mem, 1)
        total = keep + swap(send, "mem", n_mem, 1)
        sums = {2 * i: total[i * own : (i + 1) * own] for i in range(half_count)}
        for reach in reversed(rounds):
            gone = 0
            for mask in reach:
                gone |= mask
            stay = {j: [v] for j, v in sums.items() if not j & gone}
            for mask in reach:
                for j in stay:
                    stay[j].append(swap(sums[j ^ mask], "mem", n_mem, mask))
            sums = {j: sum(v[1:], v[0]) for j, v in stay.items()}
        gain_table = sums[0].T / points
        final_cover = final(ids, final_half, final_other, emb, scaling)
        return gain_table, final_cover

    return per_device


def solution(mesh):
    placed = (P(("grp", "mem"), None), P("grp", "mem"), P("grp", None), P())
    body = build(mesh.shape["grp"], mesh.shape["mem"])

    return jax.shard_map(
        body,
        mesh=mesh,
        in_specs=placed,
        out_specs=(P("grp", "mem"), P(("grp", "mem"))),
        check_vma=False,
    )
```

time: 75.8 us -> 34.7 us (0.46)
  blocking collectives: 51.1 us -> 0 us
  starting transfers between devices: 0 us -> 14 us
  matrix products: 14.1 us -> 0.25 us
  Pallas kernels: 0 us -> 10.2 us
  other arithmetic: 5.58 us -> 0.7 us
  waiting for transfers between devices: 0 us -> 4.15 us
  local copies, waits for them, and re-layouts: 2.9 us -> 4.31 us
    all_gather x2 -> x0, blocking collectives: 27.5 us -> none  [the longest x1 16.2 us: per_device(): union_rows = lax.all_gather(winners, 'grp', axis=0, tiled=True)]
    unnamed x1 -> x0, blocking collectives: 23.6 us -> none
    ppermute x0 -> x15, starting transfers between devices: none -> 14 us  [swap(): return lax.ppermute(x, axis, [(i, i ^ mask) for i in range(size)])]
    dot_general x4 -> x1, matrix products: 14.1 us -> 0.25 us  [per_device(): jnp.dot(table, part, preferred_element_type=jnp.float32).astype(emb.dtype)]
    pallas_call x0 -> x4, Pallas kernels: none -> 10.2 us  [the longest x1 3.7 us: gains(): pl.pallas_call(body, compiler_params=PARAMS, out_shape=[jax.ShapeDtypeStr...]
    ppermute x0 -> x15, waiting for transfers between devices: none -> 4.15 us  [swap(): return lax.ppermute(x, axis, [(i, i ^ mask) for i in range(size)])]
    reduce_sum x16 -> x0, other arithmetic: 3.49 us -> none  [greedy_step(): jnp.sum(jnp.maximum(similar_map - cover_now[:, None], 0.0), axis=0)]
    unnamed x7 -> x15, local copies, waits for them, and re-layouts: 1.26 us -> 4.3 us
  transfers between devices with their start and end apart: 0 -> 15, of which waited for: 0 -> 6; matrix products, arithmetic and copies ran while one was open for 0% -> 5% of each run, Pallas kernels for 0% -> 2%
where the time goes in v1:
time: 34.7 us; the launch traced here: 34.5 us
  starting transfers between devices  14 us (40%)
  Pallas kernels  10.2 us (29%)
  local copies, waits for them, and re-layouts  4.31 us (12%)
  waiting for transfers between devices  4.15 us (12%)
  between operations  0.79 us (2%)
  other arithmetic  0.7 us (2%)
    ppermute x15, starting transfers between devices, swap(): return lax.ppermute(x, axis, [(i, i ^ mask) for i in range(size)])  14 us
    unnamed x15, local copies, waits for them, and re-layouts  4.3 us
    ppermute x15, waiting for transfers between devices, swap(): return lax.ppermute(x, axis, [(i, i ^ mask) for i in range(size)])  4.15 us
    pallas_call x1, Pallas kernels, gains(): pl.pallas_call(body, compiler_params=PARAMS, out_shape=[jax.ShapeDtypeStr...  3.7 us
    pallas_call x1, Pallas kernels, final(): pl.pallas_call(body, compiler_params=PARAMS, out_shape=jax.ShapeDtypeStru...  3.43 us
    pallas_call x1, Pallas kernels, pick_rows(): pl.pallas_call(pick_kernel, compiler_params=pltpu.CompilerParams(vmem_lim...  2.44 us
  transfers between devices with their start and end apart: 15, of which 6 were waited for; matrix products, arithmetic and copies ran while one was open for 5% of the time, Pallas kernels for 2%

profile of v1, /device:TPU:0, one launch (start us, length us, event | category | flops | bytes accessed | tf_op | source)
XLA Modules:
  0.0 34.5 jit_solution(9857742791165686168)
XLA Ops:
  0.7 0.1 pad_add_fusion.refs_0_
  0.7 2.4 %shard_map.59.refs_3_ = bf16[8,4096]{1,0:T(8,128)(2,1)} custom-call(s32[1,8]{1,0:T(1,128)} %picks_ref, bf16[1024,4096]{1,0:T(8,128)(2,1)} %refs_3_.3), custom_call_target="tpu_custom_call" | custom-call | tf_op jit(solution)/shard_map/pallas_call | solution.py:37
  3.2 0.6 %collective-permute-start.3 = (bf16[8,4096]{1,0:T(8,128)(2,1)}, bf16[8,4096]{1,0:T(8,128)(2,1)S(1)}, u32[]{:S(2)}, u32[]{:S(2)}) collective-permute-start(bf16[8,4096]{1,0:T(8,128)(2,1)} %shard_map.59.refs_3_), channel_id=1, source_target_pairs={{0,1},{1,0},{2,3},{3,2},{4,5},{5,4},{6,7},{7,6},{8,9},{9,8},{10,11... | collective-permute-start | bytes 196616 | tf_op jit(solution)/shard_map/ppermute | solution.py:147
  3.8 3.5 %collective-permute-start.2 = (bf16[8,4096]{1,0:T(8,128)(2,1)}, bf16[8,4096]{1,0:T(8,128)(2,1)S(1)}, u32[]{:S(2)}, u32[]{:S(2)}) collective-permute-start(bf16[8,4096]{1,0:T(8,128)(2,1)} %shard_map.59.refs_3_), channel_id=1, source_target_pairs={{0,6},{1,7},{2,4},{3,5},{4,2},{5,3},{6,0},{7,1},{8,14},{9,15},{10,... | collective-permute-start | bytes 196616 | tf_op jit(solution)/shard_map/ppermute | solution.py:147
  7.3 0.5 %collective-permute-start.1 = (bf16[8,4096]{1,0:T(8,128)(2,1)}, bf16[8,4096]{1,0:T(8,128)(2,1)S(1)}, u32[]{:S(2)}, u32[]{:S(2)}) collective-permute-start(bf16[8,4096]{1,0:T(8,128)(2,1)} %shard_map.59.refs_3_), channel_id=1, source_target_pairs={{0,4},{1,5},{2,6},{3,7},{4,0},{5,1},{6,2},{7,3},{8,12},{9,13},{10,... | collective-permute-start | bytes 196616 | tf_op jit(solution)/shard_map/ppermute | solution.py:147
  7.8 0.1 collective-permute-start
  7.9 0.9 %constant_dynamic-update-slice_fusion.7 = bf16[64,4096]{1,0:T(8,128)(2,1)S(1)} fusion(bf16[8,4096]{1,0:T(8,128)(2,1)} %shard_map.59.refs_3_), kind=kLoop, calls=%fused_computation.10 | loop fusion | bytes 131072
  8.8 0.0 copy-start
  8.8 3.4 %copy-done = bf16[1024,4096]{1,0:T(8,128)(2,1)S(1)} copy-done((bf16[1024,4096]{1,0:T(8,128)(2,1)S(1)}, bf16[1024,4096]{1,0:T(8,128)(2,1)}, u32[]{:S(2)}) %copy-start) | copy-done | bytes 8388632
  12.2 0.7 %shard_map.61 = bf16[16,64]{1,0:T(8,128)(2,1)S(1)} custom-call(s32[2]{0:T(128)S(1)} %pad_add_fusion.refs_0_, s32[1,16]{1,0:T(1,128)S(1)} %copy-done.3, s32[16]{0:T(128)S(1)} %copy-done.2, bf16[1024,4096]{1,0:T(8,128)(2,1)S(1)} %copy-done), custom_call_target="tpu_custom_call" | custom-call | tf_op jit(solution)/shard_map/pallas_call | solution.py:68
  12.9 0.0 collective-permute-done.2.refs_6_
  12.9 0.1 collective-permute-start.6
  12.9 0.0 collective-permute-done.1.refs_5_
  13.0 0.5 %collective-permute-start.5 = (bf16[8,4096]{1,0:T(8,128)(2,1)S(1)}, bf16[8,4096]{1,0:T(8,128)(2,1)S(1)}, u32[]{:S(2)}, u32[]{:S(2)}) collective-permute-start(bf16[8,4096]{1,0:T(8,128)(2,1)S(1)} %collective-permute-done.1.refs_5_), channel_id=1, source_target_pairs={{0,1},{1,0},{2,3},{3,2},{4,5},{5,4},{6,7},{7,6},{8,9},{9,8},{10,11... | collective-permute-start | bytes 196616 | tf_op jit(solution)/shard_map/ppermute | solution.py:147
  13.5 0.1 collective-permute-start.4
  13.6 0.6 %collective-permute-done.6.refs_10_ = bf16[8,4096]{1,0:T(8,128)(2,1)S(1)} collective-permute-done((bf16[8,4096]{1,0:T(8,128)(2,1)S(1)}, bf16[8,4096]{1,0:T(8,128)(2,1)S(1)}, u32[]{:S(2)}, u32[]{:S(2)}) %collective-permute-start.6) | collective-permute-done | bytes 65568 | tf_op jit(solution)/shard_map/ppermute | solution.py:147
  14.2 0.2 collective-permute-done.5.refs_9_
  14.4 0.4 %collective-permute-done.4.refs_8_ = bf16[8,4096]{1,0:T(8,128)(2,1)S(1)} collective-permute-done((bf16[8,4096]{1,0:T(8,128)(2,1)S(1)}, bf16[8,4096]{1,0:T(8,128)(2,1)S(1)}, u32[]{:S(2)}, u32[]{:S(2)}) %collective-permute-start.4) | collective-permute-done | bytes 65568 | tf_op jit(solution)/shard_map/ppermute | solution.py:147
  14.7 3.7 %shard_map.60 = (f32[32,16]{1,0:T(8,128)S(1)}, f32[32,16]{1,0:T(8,128)S(1)}) custom-call(s32[2]{0:T(128)S(1)} %pad_add_fusion.refs_0_, s32[1,16]{1,0:T(1,128)S(1)} %copy-done.3, bf16[1024,4096]{1,0:T(8,128)(2,1)S(1)} %copy-done, bf16[8,4096]{1,0:T(8,128)(2,1)S(1)} %copy-done.1, bf16[8,4096]{1,0:T(8,128)(2,1)S(1)} %collective-permute-done.refs_4_, ...), custom_call_target="tpu_custom_call" | custom-call | flops 4294967296 | bytes 8388608 | tf_op jit(solution)/shard_map/pallas_call | solution.py:106
  18.4 0.2 collective-permute-start.7
  18.7 0.3 convolution_convert_fusion
  18.9 4.0 %collective-permute-start.13 = (bf16[16,2048]{1,0:T(8,128)(2,1)S(1)}, bf16[16,2048]{1,0:T(8,128)(2,1)S(1)}, u32[]{:S(2)}, u32[]{:S(2)}) collective-permute-start(bf16[16,2048]{1,0:T(8,128)(2,1)S(1)} %convolution_convert_fusion), channel_id=1, source_target_pairs={{0,24},{8,16},{16,8},{24,0},{1,25},{9,17},{17,9},{25,1},{2,26},{10... | collective-permute-start | bytes 196616 | tf_op jit(solution)/shard_map/ppermute | solution.py:147
  23.0 0.6 %collective-permute-start.11 = (bf16[16,2048]{1,0:T(8,128)(2,1)S(1)}, bf16[16,2048]{1,0:T(8,128)(2,1)S(1)}, u32[]{:S(2)}, u32[]{:S(2)}) collective-permute-start(bf16[16,2048]{1,0:T(8,128)(2,1)S(1)} %convolution_convert_fusion), channel_id=1, source_target_pairs={{0,8},{8,0},{16,24},{24,16},{1,9},{9,1},{17,25},{25,17},{2,10},{10... | collective-permute-start | bytes 196616 | tf_op jit(solution)/shard_map/ppermute | solution.py:147
  23.6 1.7 %collective-permute-start.8 = (f32[8,16]{1,0:T(8,128)S(1)}, f32[8,16]{1,0:T(8,128)S(1)}, u32[]{:S(2)}, u32[]{:S(2)}) collective-permute-start(f32[8,16]{1,0:T(8,128)S(1)} %get-tuple-element.12), channel_id=1, source_target_pairs={{0,2},{1,3},{2,0},{3,1},{4,6},{5,7},{6,4},{7,5},{8,10},{9,11},{10,... | collective-permute-start | bytes 1544 | tf_op jit(solution)/shard_map/ppermute | solution.py:147
  25.3 1.5 %collective-permute-start.10 = (f32[8,16]{1,0:T(8,128)S(1)}, f32[8,16]{1,0:T(8,128)S(1)}, u32[]{:S(2)}, u32[]{:S(2)}) collective-permute-start(f32[8,16]{1,0:T(8,128)S(1)} %get-tuple-element.13), channel_id=1, source_target_pairs={{0,6},{1,7},{2,4},{3,5},{4,2},{5,3},{6,0},{7,1},{8,14},{9,15},{10,... | collective-permute-start | bytes 1544 | tf_op jit(solution)/shard_map/ppermute | solution.py:147
  26.8 0.5 %collective-permute-start.9 = (f32[8,16]{1,0:T(8,128)S(1)}, f32[8,16]{1,0:T(8,128)S(1)}, u32[]{:S(2)}, u32[]{:S(2)}) collective-permute-start(f32[8,16]{1,0:T(8,128)S(1)} %get-tuple-element.14), channel_id=1, source_target_pairs={{0,4},{1,5},{2,6},{3,7},{4,0},{5,1},{6,2},{7,3},{8,12},{9,13},{10,... | collective-permute-start | bytes 1544 | tf_op jit(solution)/shard_map/ppermute | solution.py:147
  27.3 1.6 %collective-permute-done.12 = bf16[16,2048]{1,0:T(8,128)(2,1)S(1)} collective-permute-done((bf16[16,2048]{1,0:T(8,128)(2,1)S(1)}, bf16[16,2048]{1,0:T(8,128)(2,1)S(1)}, u32[]{:S(2)}, u32[]{:S(2)}) %collective-permute-start.12) | collective-permute-done | bytes 65568 | tf_op jit(solution)/shard_map/ppermute | solution.py:147
  29.0 0.1 collective-permute-start.14
  29.1 0.8 %collective-permute-done.10 = f32[8,16]{1,0:T(8,128)S(1)} collective-permute-done((f32[8,16]{1,0:T(8,128)S(1)}, f32[8,16]{1,0:T(8,128)S(1)}, u32[]{:S(2)}, u32[]{:S(2)}) %collective-permute-start.10) | collective-permute-done | bytes 544 | tf_op jit(solution)/shard_map/ppermute | solution.py:147
  29.8 0.6 %collective-permute-done.9 = f32[8,16]{1,0:T(8,128)S(1)} collective-permute-done((f32[8,16]{1,0:T(8,128)S(1)}, f32[8,16]{1,0:T(8,128)S(1)}, u32[]{:S(2)}, u32[]{:S(2)}) %collective-permute-start.9) | collective-permute-done | bytes 544 | tf_op jit(solution)/shard_map/ppermute | solution.py:147
  30.4 0.6 %fusion.4 = f32[16,8]{0,1:T(8,128)} fusion(f32[8,16]{1,0:T(8,128)S(1)} %collective-permute-done.10, f32[8,16]{1,0:T(8,128)S(1)} %collective-permute-done.9, f32[8,16]{1,0:T(8,128)S(1)} %collective-permute-done.8, f32[32,16]{1,0:T(8,128)S(1)} %add.24), kind=kLoop, calls=%fused_computation.15 | loop fusion | flops 512 | bytes 2560 | tf_op jit(solution)/shard_map/div | solution.py:198
  31.0 3.4 %shard_map.62 = f32[1024]{0:T(1024)} custom-call(s32[2]{0:T(128)S(1)} %pad_add_fusion.refs_0_, bf16[16,2048]{1,0:T(8,128)(2,1)S(1)} %add_add_fusion.refs_1_, bf16[16,2048]{1,0:T(8,128)(2,1)S(1)} %collective-permute-done.14.refs_2_, bf16[1024,4096]{1,0:T(8,128)(2,1)S(1)} %copy-done), custom_call_target="tpu_custom_call" | custom-call | flops 4294967296 | bytes 8388608 | tf_op jit(solution)/shard_map/pallas_call | solution.py:132
  (24 shorter events, 0.1 us)
Async XLA Ops:
  0.6 8.2 %copy-start.3 = (s32[1,16]{1,0:T(1,128)S(1)}, s32[1,16]{1,0:T(1,128)}, u32[]{:S(2)}) copy-start(s32[1,16]{1,0:T(1,128)} %refs_1_.3) | copy-start | bytes 196
  0.6 8.1 %copy-start.2 = (s32[16]{0:T(128)S(1)}, s32[16]{0:T(128)}, u32[]{:S(2)}) copy-start(s32[16]{0:T(128)} %refs_2_.3) | copy-start | bytes 196
  3.2 11.5 %copy-start.1 = (bf16[8,4096]{1,0:T(8,128)(2,1)S(1)}, bf16[8,4096]{1,0:T(8,128)(2,1)}, u32[]{:S(2)}) copy-start(bf16[8,4096]{1,0:T(8,128)(2,1)} %shard_map.59.refs_3_) | copy-start | bytes 196612
  3.2 10.4 %collective-permute-start.3 = (bf16[8,4096]{1,0:T(8,128)(2,1)}, bf16[8,4096]{1,0:T(8,128)(2,1)S(1)}, u32[]{:S(2)}, u32[]{:S(2)}) collective-permute-start(bf16[8,4096]{1,0:T(8,128)(2,1)} %shard_map.59.refs_3_), channel_id=1, source_target_pairs={{0,1},{1,0},{2,3},{3,2},{4,5},{5,4},{6,7},{7,6},{8,9},{9,8},{10,11... | collective-permute-start | bytes 196616 | tf_op jit(solution)/shard_map/ppermute | solution.py:147
  3.8 9.1 %collective-permute-start.2 = (bf16[8,4096]{1,0:T(8,128)(2,1)}, bf16[8,4096]{1,0:T(8,128)(2,1)S(1)}, u32[]{:S(2)}, u32[]{:S(2)}) collective-permute-start(bf16[8,4096]{1,0:T(8,128)(2,1)} %shard_map.59.refs_3_), channel_id=1, source_target_pairs={{0,6},{1,7},{2,4},{3,5},{4,2},{5,3},{6,0},{7,1},{8,14},{9,15},{10,... | collective-permute-start | bytes 196616 | tf_op jit(solution)/shard_map/ppermute | solution.py:147
  7.3 5.7 %collective-permute-start.1 = (bf16[8,4096]{1,0:T(8,128)(2,1)}, bf16[8,4096]{1,0:T(8,128)(2,1)S(1)}, u32[]{:S(2)}, u32[]{:S(2)}) collective-permute-start(bf16[8,4096]{1,0:T(8,128)(2,1)} %shard_map.59.refs_3_), channel_id=1, source_target_pairs={{0,4},{1,5},{2,6},{3,7},{4,0},{5,1},{6,2},{7,3},{8,12},{9,13},{10,... | collective-permute-start | bytes 196616 | tf_op jit(solution)/shard_map/ppermute | solution.py:147
  7.8 5.7 %collective-permute-start = (bf16[8,4096]{1,0:T(8,128)(2,1)}, bf16[8,4096]{1,0:T(8,128)(2,1)S(1)}, u32[]{:S(2)}, u32[]{:S(2)}) collective-permute-start(bf16[8,4096]{1,0:T(8,128)(2,1)} %shard_map.59.refs_3_), channel_id=1, source_target_pairs={{0,2},{1,3},{2,0},{3,1},{4,6},{5,7},{6,4},{7,5},{8,10},{9,11},{10,... | collective-permute-start | bytes 196616 | tf_op jit(solution)/shard_map/ppermute | solution.py:147
  8.8 3.4 %copy-start = (bf16[1024,4096]{1,0:T(8,128)(2,1)S(1)}, bf16[1024,4096]{1,0:T(8,128)(2,1)}, u32[]{:S(2)}) copy-start(bf16[1024,4096]{1,0:T(8,128)(2,1)} %refs_3_.3) | copy-start | bytes 25165828
  12.9 1.3 %collective-permute-start.6 = (bf16[8,4096]{1,0:T(8,128)(2,1)S(1)}, bf16[8,4096]{1,0:T(8,128)(2,1)S(1)}, u32[]{:S(2)}, u32[]{:S(2)}) collective-permute-start(bf16[8,4096]{1,0:T(8,128)(2,1)S(1)} %collective-permute-done.2.refs_6_), channel_id=1, source_target_pairs={{0,1},{1,0},{2,3},{3,2},{4,5},{5,4},{6,7},{7,6},{8,9},{9,8},{10,11... | collective-permute-start | bytes 196616 | tf_op jit(solution)/shard_map/ppermute | solution.py:147
  13.0 1.4 %collective-permute-start.5 = (bf16[8,4096]{1,0:T(8,128)(2,1)S(1)}, bf16[8,4096]{1,0:T(8,128)(2,1)S(1)}, u32[]{:S(2)}, u32[]{:S(2)}) collective-permute-start(bf16[8,4096]{1,0:T(8,128)(2,1)S(1)} %collective-permute-done.1.refs_5_), channel_id=1, source_target_pairs={{0,1},{1,0},{2,3},{3,2},{4,5},{5,4},{6,7},{7,6},{8,9},{9,8},{10,11... | collective-permute-start | bytes 196616 | tf_op jit(solution)/shard_map/ppermute | solution.py:147
  13.5 1.3 %collective-permute-start.4 = (bf16[8,4096]{1,0:T(8,128)(2,1)S(1)}, bf16[8,4096]{1,0:T(8,128)(2,1)S(1)}, u32[]{:S(2)}, u32[]{:S(2)}) collective-permute-start(bf16[8,4096]{1,0:T(8,128)(2,1)S(1)} %collective-permute-done.refs_4_), channel_id=1, source_target_pairs={{0,1},{1,0},{2,3},{3,2},{4,5},{5,4},{6,7},{7,6},{8,9},{9,8},{10,11... | collective-permute-start | bytes 196616 | tf_op jit(solution)/shard_map/ppermute | solution.py:147
  18.4 5.2 %collective-permute-start.7 = (f32[32,16]{1,0:T(8,128)S(1)}, f32[32,16]{1,0:T(8,128)S(1)}, u32[]{:S(2)}, u32[]{:S(2)}) collective-permute-start(f32[32,16]{1,0:T(8,128)S(1)} %get-tuple-element.10), channel_id=1, source_target_pairs={{0,1},{1,0},{2,3},{3,2},{4,5},{5,4},{6,7},{7,6},{8,9},{9,8},{10,11... | collective-permute-start | bytes 6152 | tf_op jit(solution)/shard_map/ppermute | solution.py:147
  18.9 7.9 %collective-permute-start.13 = (bf16[16,2048]{1,0:T(8,128)(2,1)S(1)}, bf16[16,2048]{1,0:T(8,128)(2,1)S(1)}, u32[]{:S(2)}, u32[]{:S(2)}) collective-permute-start(bf16[16,2048]{1,0:T(8,128)(2,1)S(1)} %convolution_convert_fusion), channel_id=1, source_target_pairs={{0,24},{8,16},{16,8},{24,0},{1,25},{9,17},{17,9},{25,1},{2,26},{10... | collective-permute-start | bytes 196616 | tf_op jit(solution)/shard_map/ppermute | solution.py:147
  23.0 6.0 %collective-permute-start.12 = (bf16[16,2048]{1,0:T(8,128)(2,1)S(1)}, bf16[16,2048]{1,0:T(8,128)(2,1)S(1)}, u32[]{:S(2)}, u32[]{:S(2)}) collective-permute-start(bf16[16,2048]{1,0:T(8,128)(2,1)S(1)} %convolution_convert_fusion), channel_id=1, source_target_pairs={{0,16},{8,24},{16,0},{24,8},{1,17},{9,25},{17,1},{25,9},{2,18},{10... | collective-permute-start | bytes 196616 | tf_op jit(solution)/shard_map/ppermute | solution.py:147
  23.0 6.0 %collective-permute-start.11 = (bf16[16,2048]{1,0:T(8,128)(2,1)S(1)}, bf16[16,2048]{1,0:T(8,128)(2,1)S(1)}, u32[]{:S(2)}, u32[]{:S(2)}) collective-permute-start(bf16[16,2048]{1,0:T(8,128)(2,1)S(1)} %convolution_convert_fusion), channel_id=1, source_target_pairs={{0,8},{8,0},{16,24},{24,16},{1,9},{9,1},{17,25},{25,17},{2,10},{10... | collective-permute-start | bytes 196616 | tf_op jit(solution)/shard_map/ppermute | solution.py:147
  23.6 5.4 %collective-permute-start.8 = (f32[8,16]{1,0:T(8,128)S(1)}, f32[8,16]{1,0:T(8,128)S(1)}, u32[]{:S(2)}, u32[]{:S(2)}) collective-permute-start(f32[8,16]{1,0:T(8,128)S(1)} %get-tuple-element.12), channel_id=1, source_target_pairs={{0,2},{1,3},{2,0},{3,1},{4,6},{5,7},{6,4},{7,5},{8,10},{9,11},{10,... | collective-permute-start | bytes 1544 | tf_op jit(solution)/shard_map/ppermute | solution.py:147
  25.3 4.5 %collective-permute-start.10 = (f32[8,16]{1,0:T(8,128)S(1)}, f32[8,16]{1,0:T(8,128)S(1)}, u32[]{:S(2)}, u32[]{:S(2)}) collective-permute-start(f32[8,16]{1,0:T(8,128)S(1)} %get-tuple-element.13), channel_id=1, source_target_pairs={{0,6},{1,7},{2,4},{3,5},{4,2},{5,3},{6,0},{7,1},{8,14},{9,15},{10,... | collective-permute-start | bytes 1544 | tf_op jit(solution)/shard_map/ppermute | solution.py:147
  26.8 3.6 %collective-permute-start.9 = (f32[8,16]{1,0:T(8,128)S(1)}, f32[8,16]{1,0:T(8,128)S(1)}, u32[]{:S(2)}, u32[]{:S(2)}) collective-permute-start(f32[8,16]{1,0:T(8,128)S(1)} %get-tuple-element.14), channel_id=1, source_target_pairs={{0,4},{1,5},{2,6},{3,7},{4,0},{5,1},{6,2},{7,3},{8,12},{9,13},{10,... | collective-permute-start | bytes 1544 | tf_op jit(solution)/shard_map/ppermute | solution.py:147
  29.0 2.1 %collective-permute-start.14 = (bf16[16,2048]{1,0:T(8,128)(2,1)S(1)}, bf16[16,2048]{1,0:T(8,128)(2,1)S(1)}, u32[]{:S(2)}, u32[]{:S(2)}) collective-permute-start(bf16[16,2048]{1,0:T(8,128)(2,1)S(1)} %add_add_fusion.refs_1_), channel_id=1, source_target_pairs={{0,1},{1,0},{2,3},{3,2},{4,5},{5,4},{6,7},{7,6},{8,9},{9,8},{10,11... | collective-permute-start | bytes 196616 | tf_op jit(solution)/shard_map/ppermute | solution.py:147
